TPU v7x, 128 devices: a whole 4x4x4 slice. The times are simulated.
128 devices in a mesh: gx: 8 (over z, x_lo), gy: 16 (over x_hi, y, core).
Axes of the slice: x: 4 (x_hi: 2, x_lo: 2; x = x_hi * 2 + x_lo), y: 4, z: 4, core: 2. Of those that a mesh axis runs over, the one named last changes fastest.
Arguments:
- fields: float32 [6, 256, 512, 128], P(None, 'gx', 'gy'), may hold values from -6 to 6
- eps_background: float32 [256, 512, 128], P('gx', 'gy'), may hold values from 1 to 4
- target: float32 [256, 256], replicated, may hold values from 1 to 10
- widths: float32 [16384], P(('gx', 'gy')), may hold values from 0.2 to 1
- intersection: float32 [16384, 16], P(('gx', 'gy')), may hold values from 0.1 to 1
- pillar_tile: int32 [16384, 1], P(('gx', 'gy')), may hold values from 0 to 127; in each aligned block of 128 rows (0 to 127, 128 to 255, ...) at most 2 rows name the same one
- anchors: int32 [16384, 2], P(('gx', 'gy')), may hold values from 0 to 28
Outputs:
- final_fields: float32 [6, 256, 512, 128], P(None, 'gx', 'gy')
- focal_power: float32 [256, 256], P(('gx', 'gy'))
- grad_widths: float32 [16384], P(('gx', 'gy'))
Inputs may be any that keep to these rules, and one draw needn't show every extreme that they name: `pillar_tile`: in the pillars of one device (aligned blocks of 128), no tile is named by more than 2 pillars, a bound that some block reaches. Tile t is the one at gx index t div (512 div 32) and gy index t mod (512 div 32).
All inputs are finite; a program needn't handle non-finite values.
Results may differ from a plain program's by a relative error of at most 0.00016.
Values sent between devices are 32-bit elements; how exact they have to be, the bound alone decides.
A program may use at most 128 MiB of HBM per device.

v0:
```python
import math
import jax
import jax.numpy as jnp
from jax import lax
from jax.sharding import PartitionSpec as P

TILE = 32
P_DEV = 128
NT = 4
ZP = 4
U = 256
V = 256
ZM = 64
COURANT = 0.5
ANGULAR_STEP = 0.9
DELTA_EPS = 4.0


def passed_along(shard, axis, by):
    count = lax.axis_size(axis)
    pairs = [(i, i + by) for i in range(count) if 0 <= i + by < count]
    return lax.ppermute(shard, axis, pairs)


def plus_diff(field, rim_layer, axis):
    extended = jnp.concatenate([field, rim_layer], axis=axis)
    return lax.slice_in_dim(extended, 1, extended.shape[axis], axis=axis) - field


def minus_diff(field, rim_layer, axis):
    extended = jnp.concatenate([rim_layer, field], axis=axis)
    return field - lax.slice_in_dim(extended, 0, field.shape[axis], axis=axis)


def leap_step(fields_now, inv_eps, sources):
    elec_x, elec_y, elec_z, magn_x, magn_y, magn_z = fields_now
    z_blank = jnp.zeros_like(elec_x[:, :, :1])
    rim_east = passed_along(jnp.stack([elec_y[:1], elec_z[:1]]), "gx", -1)
    rim_north = passed_along(jnp.stack([elec_x[:, :1], elec_z[:, :1]]), "gy", -1)
    curl_x = plus_diff(elec_z, rim_north[1], 1) - plus_diff(elec_y, z_blank, 2)
    curl_y = plus_diff(elec_x, z_blank, 2) - plus_diff(elec_z, rim_east[1], 0)
    curl_z = plus_diff(elec_y, rim_east[0], 0) - plus_diff(elec_x, rim_north[0], 1)
    magn_x = magn_x - COURANT * curl_x
    magn_y = magn_y - COURANT * curl_y
    magn_z = magn_z - COURANT * curl_z
    rim_west = passed_along(jnp.stack([magn_y[-1:], magn_z[-1:]]), "gx", 1)
    rim_south = passed_along(jnp.stack([magn_x[:, -1:], magn_z[:, -1:]]), "gy", 1)
    curl_x = minus_diff(magn_z, rim_south[1], 1) - minus_diff(magn_y, z_blank, 2)
    curl_y = minus_diff(magn_x, z_blank, 2) - minus_diff(magn_z, rim_west[1], 0)
    curl_z = minus_diff(magn_y, rim_west[0], 0) - minus_diff(magn_x, rim_south[0], 1)
    elec_x = elec_x + COURANT * (curl_x - sources[0]) * inv_eps
    elec_y = elec_y + COURANT * (curl_y - sources[1]) * inv_eps
    elec_z = elec_z + COURANT * curl_z * inv_eps
    return (elec_x, elec_y, elec_z, magn_x, magn_y, magn_z)


def kernel_table(count_out, count_in, offset, length):
    focal_pos = (jnp.arange(count_out, dtype=jnp.float32) + 0.5) / count_out - 0.5
    cell_pos = (
        offset.astype(jnp.float32) + jnp.arange(length, dtype=jnp.float32) + 0.5
    ) / count_in - 0.5
    phase = math.pi * count_out * (focal_pos[:, None] - cell_pos[None, :]) ** 2
    return (jnp.cos(phase), jnp.sin(phase))


def contract(pattern, first_op, second_op):
    return jnp.einsum(pattern, first_op, second_op, precision=lax.Precision.HIGHEST)


def project_forward(mon_re, mon_im, table_x, table_y, norm_scale):
    x_re, x_im = table_x
    y_re, y_im = table_y
    part_re = contract("ux,cxy->cuy", x_re, mon_re) - contract("ux,cxy->cuy", x_im, mon_im)
    part_im = contract("ux,cxy->cuy", x_re, mon_im) + contract("ux,cxy->cuy", x_im, mon_re)
    far_re = contract("cuy,vy->cuv", part_re, y_re) - contract("cuy,vy->cuv", part_im, y_im)
    far_im = contract("cuy,vy->cuv", part_re, y_im) + contract("cuy,vy->cuv", part_im, y_re)
    return norm_scale * jnp.stack([far_re, far_im])


def project_back(weighted, table_x, table_y, norm_scale):
    x_re, x_im = table_x
    y_re, y_im = table_y
    w_re = weighted[0]
    w_im = weighted[1]
    half_re = contract("cuv,vy->cuy", w_re, y_re) - contract("cuv,vy->cuy", w_im, y_im)
    half_im = contract("cuv,vy->cuy", w_re, y_im) + contract("cuv,vy->cuy", w_im, y_re)
    back_re = contract("ux,cuy->cxy", x_re, half_re) - contract("ux,cuy->cxy", x_im, half_im)
    back_im = contract("ux,cuy->cxy", x_re, half_im) + contract("ux,cuy->cxy", x_im, half_re)
    return (2.0 * norm_scale * back_re, 2.0 * norm_scale * back_im)


def shards(fields, eps_background, target, widths, intersection, pillar_tile, anchors):
    span_x = lax.axis_size("gx")
    span_y = lax.axis_size("gy")
    devices = span_x * span_y
    place_x = lax.axis_index("gx")
    place_y = lax.axis_index("gy")
    linear = place_x * span_y + place_y
    offsets = jnp.arange(16, dtype=jnp.int32)
    capacity = 2 * max(1, P_DEV // devices)
    target_tile = pillar_tile[:, 0]
    onehot = (target_tile[:, None] == jnp.arange(devices, dtype=jnp.int32)[None, :]).astype(
        jnp.int32
    )
    earlier = jnp.cumsum(onehot, axis=0) - onehot
    order_in = jnp.sum(earlier * onehot, axis=1)
    slot_ids = target_tile * capacity + order_in
    packed = (
        jnp.zeros((devices * capacity, 16), jnp.float32)
        .at[slot_ids]
        .set(intersection * widths[:, None])
    )
    packed_at = (
        jnp.zeros((devices * capacity, 2), jnp.float32)
        .at[slot_ids]
        .set(anchors.astype(jnp.float32))
    )
    got_vals, got_at = (
        lax.all_to_all(
            packed.reshape(devices, capacity, 16),
            ("gx", "gy"),
            split_axis=0,
            concat_axis=0,
            tiled=True,
        ),
        lax.all_to_all(
            packed_at.reshape(devices, capacity, 2),
            ("gx", "gy"),
            split_axis=0,
            concat_axis=0,
            tiled=True,
        ),
    )
    local_vals = got_vals.reshape(devices * capacity, 16)
    local_at = got_at.reshape(devices * capacity, 2).astype(jnp.int32)
    cells_x = local_at[:, 0:1] + (offsets // 4)[None, :]
    cells_y = local_at[:, 1:2] + (offsets % 4)[None, :]
    filling = jnp.zeros((TILE, TILE), jnp.float32).at[cells_x, cells_y].add(local_vals)
    z_index = jnp.arange(fields.shape[3], dtype=jnp.int32)
    layers = ((z_index >= ZM - ZP) & (z_index < ZM)).astype(jnp.float32)
    permittivity = eps_background + DELTA_EPS * filling[:, :, None] * layers[None, None, :]
    inv_eps = 1.0 / permittivity
    blank = jnp.zeros_like(eps_background)
    fields_now = tuple((fields[component] for component in range(6)))
    mon_re = jnp.zeros((2, TILE, TILE), jnp.float32)
    mon_im = jnp.zeros((2, TILE, TILE), jnp.float32)
    changes = []
    for moment in range(1, NT + 1):
        before = fields_now[:3]
        fields_now = leap_step(fields_now, inv_eps, (blank, blank, blank))
        monitor = jnp.stack([fields_now[0][:, :, ZM], fields_now[1][:, :, ZM]])
        mon_re = mon_re + math.cos(ANGULAR_STEP * moment) * monitor
        mon_im = mon_im - math.sin(ANGULAR_STEP * moment) * monitor
        changes.append(
            tuple(
                (
                    (fields_now[component] - before[component])[:, :, ZM - ZP : ZM]
                    for component in range(3)
                )
            )
        )
    norm_scale = (TILE * span_x * TILE * span_y) ** (-0.5)
    table_x = kernel_table(U, TILE * span_x, place_x * TILE, TILE)
    table_y = kernel_table(V, TILE * span_y, place_y * TILE, TILE)
    row_count = U // devices
    row_start = linear * row_count
    partial_far = project_forward(mon_re, mon_im, table_x, table_y, norm_scale)
    far_field = lax.psum(partial_far, ("gx", "gy"))
    mine_rows = lax.dynamic_slice_in_dim(far_field, row_start, row_count, 2)
    focal_power = jnp.sum(mine_rows * mine_rows, axis=(0, 1))
    weighted = jnp.stack([target * far_field[0], -(target * far_field[1])])
    back_re, back_im = project_back(weighted, table_x, table_y, norm_scale)
    adjoint = tuple((blank for component in range(6)))
    inv_layer = inv_eps[:, :, ZM - ZP : ZM]
    grad_eps = jnp.zeros((TILE, TILE, ZP), jnp.float32)
    for moment in range(1, NT + 1):
        source_step = NT + 1 - moment
        adj_drive = (
            math.cos(ANGULAR_STEP * source_step) * back_re
            + math.sin(ANGULAR_STEP * source_step) * back_im
        )
        source_x = blank.at[:, :, ZM].set(adj_drive[0])
        source_y = blank.at[:, :, ZM].set(adj_drive[1])
        adjoint = leap_step(adjoint, inv_eps, (source_x, source_y, blank))
        change = changes[source_step - 1]
        product = (
            adjoint[0][:, :, ZM - ZP : ZM] * change[0]
            + adjoint[1][:, :, ZM - ZP : ZM] * change[1]
            + adjoint[2][:, :, ZM - ZP : ZM] * change[2]
        )
        grad_eps = grad_eps - product * inv_layer
    column_grad = jnp.sum(grad_eps, axis=2)
    picked = column_grad[cells_x, cells_y]
    returned = lax.all_to_all(
        picked.reshape(devices, capacity, 16), ("gx", "gy"), split_axis=0, concat_axis=0, tiled=True
    )
    own_vals = returned.reshape(devices * capacity, 16)[slot_ids]
    grad_widths = DELTA_EPS * jnp.sum(intersection * own_vals, axis=1)
    return (jnp.stack(fields_now), focal_power, grad_widths)


def solution(mesh):
    placed = (
        P(None, "gx", "gy", None),
        P("gx", "gy", None),
        P(),
        P(("gx", "gy")),
        P(("gx", "gy"), None),
        P(("gx", "gy"), None),
        P(("gx", "gy"), None),
    )
    return jax.shard_map(
        shards,
        mesh=mesh,
        in_specs=placed,
        out_specs=(P(None, "gx", "gy", None), P(("gx", "gy"), None), P(("gx", "gy"))),
        check_vma=False,
    )
```

profile of v0, /device:TPU:1, one launch (start us, length us, event | category | flops | bytes accessed | tf_op | source)
XLA Modules:
  0.0 479.0 jit_solution(2018501460073034488)
XLA Ops:
  7.2 1.6 collective-permute-start.16
  9.4 3.3 collective-permute-start.17
  16.8 1.5 copy.4958
  18.3 12.4 %all-to-all-start = ((f32[128,2,2]{1,2,0:T(2,128)}), f32[128,2,2]{1,2,0:T(2,128)S(1)}, u32[]{:S(2)}, u32[]{:S(2)}) async-start(f32[128,2,2]{1,2,0:T(2,128)} %copy.4958), calls=%async_computation | async-start | bytes 262144 | tf_op jit(solution)/shard_map/all_to_all | solution.py:126
  30.7 2.3 slice_bitcast_fusion.3
  34.6 3.0 collective-permute-start.1
  38.1 1.3 collective-permute-start
  40.8 1.5 scatter_custom_fusion.1
  42.3 11.5 %all-to-all-start.1 = ((f32[128,2,16]{2,1,0:T(2,128)}), f32[128,2,16]{2,1,0:T(2,128)S(1)}, u32[]{:S(2)}, u32[]{:S(2)}) async-start(f32[128,2,16]{2,1,0:T(2,128)} %bitcast.24), calls=%async_computation.1 | async-start | bytes 262144 | tf_op jit(solution)/shard_map/all_to_all | solution.py:119
  56.7 7.2 %all-to-all-done.1 = f32[128,2,16]{2,1,0:T(2,128)S(1)} async-done(((f32[128,2,16]{2,1,0:T(2,128)}), f32[128,2,16]{2,1,0:T(2,128)S(1)}, u32[]{:S(2)}, u32[]{:S(2)}) %all-to-all-start.1) | async-done | bytes 16416 | tf_op jit(solution)/shard_map/all_to_all | solution.py:119
  64.0 28.9 %scatter_custom_fusion.2 = f32[1024]{0:T(1024)S(1)} fusion(s32[4096]{0:T(1024)} %reshape.500, f32[4096]{0:T(1024)S(1)} %reshape.502, f32[]{:T(128)} %constant.251.clone.1), kind=kCustom, calls=%fused_computation.635 | custom fusion | flops 4096 | bytes 4608
  95.3 2.7 collective-permute-start.18
  98.0 2.2 collective-permute-start.19
  102.4 3.5 collective-permute-start.3
  105.9 2.6 collective-permute-start.2
  111.5 1.9 collective-permute-start.5
  114.7 1.3 collective-permute-start.4
  116.8 2.6 collective-permute-done.4
  120.0 3.1 collective-permute-start.7
  123.1 5.1 %collective-permute-start.6 = (f32[2,32,1,128]{3,1,2,0:T(8,128)S(1)}, f32[2,32,1,128]{3,1,2,0:T(8,128)S(1)}, u32[]{:S(2)}, u32[]{:S(2)}) collective-permute-start(f32[2,32,1,128]{3,1,2,0:T(8,128)S(1)} %pad_maximum_fusion.63), channel_id=1, source_target_pairs={{0,1},{1,2},{2,3},{3,4},{4,5},{5,6},{6,7},{7,8},{8,9},{9,10},{10,1... | collective-permute-start | bytes 98312 | tf_op jit(solution)/shard_map/ppermute | solution.py:22
  130.7 1.9 collective-permute-start.9
  132.6 1.3 collective-permute-start.8
  133.9 2.6 collective-permute-done.9
  137.9 2.7 collective-permute-start.11
  140.7 5.8 %collective-permute-start.10 = (f32[2,32,1,128]{3,1,2,0:T(8,128)S(1)}, f32[2,32,1,128]{3,1,2,0:T(8,128)S(1)}, u32[]{:S(2)}, u32[]{:S(2)}) collective-permute-start(f32[2,32,1,128]{3,1,2,0:T(8,128)S(1)} %pad_maximum_fusion.67), channel_id=1, source_target_pairs={{0,1},{1,2},{2,3},{3,4},{4,5},{5,6},{6,7},{7,8},{8,9},{9,10},{10,1... | collective-permute-start | bytes 98312 | tf_op jit(solution)/shard_map/ppermute | solution.py:22
  148.8 1.9 collective-permute-start.13
  150.7 1.3 collective-permute-start.12
  152.0 2.6 collective-permute-done.13
  156.1 5.4 %collective-permute-start.14 = (f32[2,32,1,128]{3,1,2,0:T(8,128)S(1)}, f32[2,32,1,128]{3,1,2,0:T(8,128)S(1)}, u32[]{:S(2)}, u32[]{:S(2)}) collective-permute-start(f32[2,32,1,128]{3,1,2,0:T(8,128)S(1)} %pad_maximum_fusion.71), channel_id=1, source_target_pairs={{0,1},{1,2},{2,3},{3,4},{4,5},{5,6},{6,7},{7,8},{8,9},{9,10},{10,1... | collective-permute-start | bytes 98312 | tf_op jit(solution)/shard_map/ppermute | solution.py:22
  161.5 3.1 collective-permute-start.15
  173.1 3.1 bitcast_dynamic-update-slice_fusion.3
  177.8 152.3 %all-reduce.45.cloned.1.call-done = f32[2,2,256,256]{3,2,1,0:T(8,128)} async-done(((f32[2,2,256,256]{3,2,1,0:T(8,128)}), f32[2,2,256,256]{3,2,1,0:T(8,128)}) %all-reduce.45.cloned.1.call-update) | async-done | bytes 1048592 | tf_op jit(solution)/shard_map/psum | solution.py:168
  330.2 1.8 fusion.284
  332.0 1.8 convolution_add_fusion.2
  334.2 1.8 fusion.286
  335.9 1.8 convolution_subtract_fusion.2
  338.9 1.3 copy.4986
  340.2 1.3 copy.4984
  341.5 3.0 fusion.94
  344.5 1.9 collective-permute-start.21
  347.1 1.5 collective-permute-start.20
  348.7 1.3 copy.4994
  349.9 1.3 copy.4992
  351.2 1.3 copy.5002
  352.5 1.3 copy.5000
  353.8 1.3 copy.5012
  356.4 4.0 fusion.98
  360.5 4.0 collective-permute-start.23
  364.5 4.2 collective-permute-start.22
  370.7 2.1 collective-permute-start.25
  372.8 1.3 collective-permute-start.24
  374.1 2.6 collective-permute-done.25
  378.1 4.0 collective-permute-start.27
  382.2 5.7 %collective-permute-start.26 = (f32[2,32,1,128]{3,1,2,0:T(8,128)S(1)}, f32[2,32,1,128]{3,1,2,0:T(8,128)S(1)}, u32[]{:S(2)}, u32[]{:S(2)}) collective-permute-start(f32[2,32,1,128]{3,1,2,0:T(8,128)S(1)} %pad_maximum_fusion.85), channel_id=1, source_target_pairs={{0,1},{1,2},{2,3},{3,4},{4,5},{5,6},{6,7},{7,8},{8,9},{9,10},{10,1... | collective-permute-start | bytes 98312 | tf_op jit(solution)/shard_map/ppermute | solution.py:22
  389.8 1.9 collective-permute-start.29
  391.7 1.3 collective-permute-start.28
  393.0 2.6 collective-permute-done.29
  397.6 2.7 collective-permute-start.31
  400.3 5.7 %collective-permute-start.30 = (f32[2,32,1,128]{3,1,2,0:T(8,128)S(1)}, f32[2,32,1,128]{3,1,2,0:T(8,128)S(1)}, u32[]{:S(2)}, u32[]{:S(2)}) collective-permute-start(f32[2,32,1,128]{3,1,2,0:T(8,128)S(1)} %pad_maximum_fusion.89), channel_id=1, source_target_pairs={{0,1},{1,2},{2,3},{3,4},{4,5},{5,6},{6,7},{7,8},{8,9},{9,10},{10,1... | collective-permute-start | bytes 98312 | tf_op jit(solution)/shard_map/ppermute | solution.py:22
  407.0 5.4 %fusion.147 = f32[32,32]{1,0:T(8,128)S(1)} fusion(f32[32,32,128]{2,1,0:T(8,128)S(1)} %copy-done.26, f32[32,32,128]{2,1,0:T(8,128)S(1)} %get-tuple-element.164, f32[1,32,128]{2,1,0:T(8,128)S(1)} %get-tuple-element.191, f32[32,32,128]{2,1,0:T(8,128)S(1)} %get-tuple-element.163, f32[32,1,128]{2,1,0:T(1,128)S(1)} %bitcast.473, ...), kind=kLoop, calls=%fused_computation.197 | loop fusion | flops 265216 | bytes 18419712 | tf_op jit(solution)/shard_map/reduce_sum | solution.py:192
  412.5 27.6 %gather_fusion = f32[4096]{0:T(1024)S(1)} fusion(f32[32,32]{0,1:T(8,128)S(1)} %copy.5037, s32[4096]{0:T(1024)S(1)} %reshape.470), kind=kCustom, calls=%fused_computation | custom fusion | bytes 65536 | tf_op jit(solution)/shard_map/gather | solution.py:193
  441.0 19.8 %all-to-all-start.2 = ((f32[128,2,16]{2,1,0:T(2,128)}), f32[128,2,16]{2,1,0:T(2,128)S(1)}, u32[]{:S(2)}, u32[]{:S(2)}) async-start(f32[128,2,16]{2,1,0:T(2,128)} %reshape.462), calls=%async_computation.2 | async-start | bytes 262144 | tf_op jit(solution)/shard_map/all_to_all | solution.py:194
  461.6 1.4 multiply_reduce_fusion.2
  463.0 8.0 %all-to-all-done.2 = f32[128,2,16]{2,1,0:T(2,128)S(1)} async-done(((f32[128,2,16]{2,1,0:T(2,128)}), f32[128,2,16]{2,1,0:T(2,128)S(1)}, u32[]{:S(2)}, u32[]{:S(2)}) %all-to-all-start.2) | async-done | bytes 16416 | tf_op jit(solution)/shard_map/all_to_all | solution.py:194
  (346 shorter events, 53.2 us)
Async XLA Ops:
  7.2 30.4 %copy-start.20 = (f32[6,32,32,128]{3,2,1,0:T(8,128)S(1)}, f32[6,32,32,128]{3,2,1,0:T(8,128)}, u32[]{:S(2)}) copy-start(f32[6,32,32,128]{3,2,1,0:T(8,128)} %param.23) | copy-start | bytes 9437188
  7.2 33.3 %copy-start.52 = (f32[128,16]{0,1:T(8,128)S(1)}, f32[128,16]{0,1:T(8,128)}, u32[]{:S(2)}) copy-start(f32[128,16]{0,1:T(8,128)} %param.27) | copy-start | bytes 24580
  7.2 33.3 %copy-start.54 = (f32[128]{0:T(128)S(1)}, f32[128]{0:T(128)}, u32[]{:S(2)}) copy-start(f32[128]{0:T(128)} %param.26) | copy-start | bytes 1540
  7.2 85.9 %collective-permute-start.16 = (f32[2,1,32,128]{3,2,1,0:T(8,128)S(1)}, f32[2,1,32,128]{3,2,1,0:T(8,128)}, u32[]{:S(2)}, u32[]{:S(2)}) collective-permute-start(f32[2,1,32,128]{3,2,1,0:T(8,128)S(1)} %stack.374), channel_id=1, source_target_pairs={{16,0},{32,16},{48,32},{64,48},{80,64},{96,80},{112,96},{17,1},{33... | collective-permute-start | bytes 98312 | tf_op jit(solution)/shard_map/ppermute | solution.py:22
  9.4 84.6 %collective-permute-start.17 = (f32[2,32,1,128]{3,1,2,0:T(8,128)}, f32[2,32,1,128]{3,1,2,0:T(8,128)}, u32[]{:S(2)}, u32[]{:S(2)}) collective-permute-start(f32[2,32,1,128]{3,1,2,0:T(8,128)} %stack.375), channel_id=1, source_target_pairs={{1,0},{2,1},{3,2},{4,3},{5,4},{6,5},{7,6},{8,7},{9,8},{10,9},{11,1... | collective-permute-start | bytes 98312 | tf_op jit(solution)/shard_map/ppermute | solution.py:22
  18.3 23.9 %all-to-all-start = ((f32[128,2,2]{1,2,0:T(2,128)}), f32[128,2,2]{1,2,0:T(2,128)S(1)}, u32[]{:S(2)}, u32[]{:S(2)}) async-start(f32[128,2,2]{1,2,0:T(2,128)} %copy.4958), calls=%async_computation | async-start | bytes 262144 | tf_op jit(solution)/shard_map/all_to_all | solution.py:126
  34.6 65.6 %collective-permute-start.1 = (f32[2,32,1,128]{3,1,2,0:T(8,128)}, f32[2,32,1,128]{3,1,2,0:T(8,128)}, u32[]{:S(2)}, u32[]{:S(2)}) collective-permute-start(f32[2,32,1,128]{3,1,2,0:T(8,128)} %pad_maximum_fusion.58), channel_id=1, source_target_pairs={{1,0},{2,1},{3,2},{4,3},{5,4},{6,5},{7,6},{8,7},{9,8},{10,9},{11,1... | collective-permute-start | bytes 98312 | tf_op jit(solution)/shard_map/ppermute | solution.py:22
  38.1 62.8 %collective-permute-start = (f32[2,1,32,128]{3,2,1,0:T(8,128)}, f32[2,1,32,128]{3,2,1,0:T(8,128)}, u32[]{:S(2)}, u32[]{:S(2)}) collective-permute-start(f32[2,1,32,128]{3,2,1,0:T(8,128)} %stack.314), channel_id=1, source_target_pairs={{16,0},{32,16},{48,32},{64,48},{80,64},{96,80},{112,96},{17,1},{33... | collective-permute-start | bytes 98312 | tf_op jit(solution)/shard_map/ppermute | solution.py:22
  42.3 21.6 %all-to-all-start.1 = ((f32[128,2,16]{2,1,0:T(2,128)}), f32[128,2,16]{2,1,0:T(2,128)S(1)}, u32[]{:S(2)}, u32[]{:S(2)}) async-start(f32[128,2,16]{2,1,0:T(2,128)} %bitcast.24), calls=%async_computation.1 | async-start | bytes 262144 | tf_op jit(solution)/shard_map/all_to_all | solution.py:119
  53.7 276.5 %all-reduce.45.cloned.1.call-start = ((), (), s32[]{:S(2)}) async-start(), calls=%async_computation.3 | async-start | bytes 2097152 | tf_op jit(solution)/shard_map/psum | solution.py:168
  95.2 14.8 %copy-start.22 = (f32[32,32,128]{2,1,0:T(8,128)}, f32[32,32,128]{2,1,0:T(8,128)S(1)}, u32[]{:S(2)}) copy-start(f32[32,32,128]{2,1,0:T(8,128)S(1)} %get-tuple-element.179) | copy-start | bytes 1572868
  95.2 14.8 %copy-start.23 = (f32[32,32,128]{2,1,0:T(8,128)}, f32[32,32,128]{2,1,0:T(8,128)S(1)}, u32[]{:S(2)}) copy-start(f32[32,32,128]{2,1,0:T(8,128)S(1)} %get-tuple-element.178) | copy-start | bytes 1572868
  95.2 14.5 %copy-start.46 = (f32[32,32,128]{2,1,0:T(8,128)S(1)}, f32[32,32,128]{2,1,0:T(8,128)}, u32[]{:S(2)}) copy-start(f32[32,32,128]{2,1,0:T(8,128)} %param.24) | copy-start | bytes 1572868
  95.2 14.5 %copy-start.53 = (f32[128]{0:T(128)S(1)}, f32[128]{0:T(128)}, u32[]{:S(2)}) copy-start(f32[128]{0:T(128)} %and_convert_fusion) | copy-start | bytes 1540
  95.3 13.2 %collective-permute-start.18 = (f32[2,32,1,128]{3,1,2,0:T(8,128)S(1)}, f32[2,32,1,128]{3,1,2,0:T(8,128)S(1)}, u32[]{:S(2)}, u32[]{:S(2)}) collective-permute-start(f32[2,32,1,128]{3,1,2,0:T(8,128)S(1)} %pad_maximum_fusion.77), channel_id=1, source_target_pairs={{0,1},{1,2},{2,3},{3,4},{4,5},{5,6},{6,7},{7,8},{8,9},{9,10},{10,1... | collective-permute-start | bytes 98312 | tf_op jit(solution)/shard_map/ppermute | solution.py:22
  98.0 11.2 %collective-permute-start.19 = (f32[2,1,32,128]{3,2,1,0:T(8,128)S(1)}, f32[2,1,32,128]{3,2,1,0:T(8,128)S(1)}, u32[]{:S(2)}, u32[]{:S(2)}) collective-permute-start(f32[2,1,32,128]{3,2,1,0:T(8,128)S(1)} %pad_maximum_fusion.78), channel_id=1, source_target_pairs={{0,16},{16,32},{32,48},{48,64},{64,80},{80,96},{96,112},{1,17},{17... | collective-permute-start | bytes 98312 | tf_op jit(solution)/shard_map/ppermute | solution.py:22
  102.4 7.7 %collective-permute-start.3 = (f32[2,1,32,128]{3,2,1,0:T(8,128)S(1)}, f32[2,1,32,128]{3,2,1,0:T(8,128)S(1)}, u32[]{:S(2)}, u32[]{:S(2)}) collective-permute-start(f32[2,1,32,128]{3,2,1,0:T(8,128)S(1)} %pad_maximum_fusion.60), channel_id=1, source_target_pairs={{0,16},{16,32},{32,48},{48,64},{64,80},{80,96},{96,112},{1,17},{17... | collective-permute-start | bytes 98312 | tf_op jit(solution)/shard_map/ppermute | solution.py:22
  105.9 4.2 collective-permute-start.2
  110.7 18.5 %copy-start.8 = (f32[32,32,128]{2,1,0:T(8,128)}, f32[32,32,128]{2,1,0:T(8,128)S(1)}, u32[]{:S(2)}) copy-start(f32[32,32,128]{2,1,0:T(8,128)S(1)} %get-tuple-element.138) | copy-start | bytes 1572868
  111.5 5.2 %collective-permute-start.5 = (f32[2,32,1,128]{3,1,2,0:T(8,128)S(1)}, f32[2,32,1,128]{3,1,2,0:T(8,128)S(1)}, u32[]{:S(2)}, u32[]{:S(2)}) collective-permute-start(f32[2,32,1,128]{3,1,2,0:T(8,128)S(1)} %pad_maximum_fusion.62), channel_id=1, source_target_pairs={{1,0},{2,1},{3,2},{4,3},{5,4},{6,5},{7,6},{8,7},{9,8},{10,9},{11,1... | collective-permute-start | bytes 98312 | tf_op jit(solution)/shard_map/ppermute | solution.py:22
  114.7 4.6 collective-permute-start.4
  120.0 8.2 %collective-permute-start.7 = (f32[2,1,32,128]{3,2,1,0:T(8,128)S(1)}, f32[2,1,32,128]{3,2,1,0:T(8,128)S(1)}, u32[]{:S(2)}, u32[]{:S(2)}) collective-permute-start(f32[2,1,32,128]{3,2,1,0:T(8,128)S(1)} %pad_maximum_fusion.64), channel_id=1, source_target_pairs={{0,16},{16,32},{32,48},{48,64},{64,80},{80,96},{96,112},{1,17},{17... | collective-permute-start | bytes 98312 | tf_op jit(solution)/shard_map/ppermute | solution.py:22
  123.1 6.1 %collective-permute-start.6 = (f32[2,32,1,128]{3,1,2,0:T(8,128)S(1)}, f32[2,32,1,128]{3,1,2,0:T(8,128)S(1)}, u32[]{:S(2)}, u32[]{:S(2)}) collective-permute-start(f32[2,32,1,128]{3,1,2,0:T(8,128)S(1)} %pad_maximum_fusion.63), channel_id=1, source_target_pairs={{0,1},{1,2},{2,3},{3,4},{4,5},{5,6},{6,7},{7,8},{8,9},{9,10},{10,1... | collective-permute-start | bytes 98312 | tf_op jit(solution)/shard_map/ppermute | solution.py:22
  129.8 17.5 %copy-start = (f32[32,32,128]{2,1,0:T(8,128)}, f32[32,32,128]{2,1,0:T(8,128)S(1)}, u32[]{:S(2)}) copy-start(f32[32,32,128]{2,1,0:T(8,128)S(1)} %get-tuple-element.162) | copy-start | bytes 1572868
  129.8 17.5 %copy-start.10 = (f32[32,32,128]{2,1,0:T(8,128)}, f32[32,32,128]{2,1,0:T(8,128)S(1)}, u32[]{:S(2)}) copy-start(f32[32,32,128]{2,1,0:T(8,128)S(1)} %get-tuple-element.161) | copy-start | bytes 1572868
  130.7 5.8 %collective-permute-start.9 = (f32[2,32,1,128]{3,1,2,0:T(8,128)S(1)}, f32[2,32,1,128]{3,1,2,0:T(8,128)S(1)}, u32[]{:S(2)}, u32[]{:S(2)}) collective-permute-start(f32[2,32,1,128]{3,1,2,0:T(8,128)S(1)} %pad_maximum_fusion.66), channel_id=1, source_target_pairs={{1,0},{2,1},{3,2},{4,3},{5,4},{6,5},{7,6},{8,7},{9,8},{10,9},{11,1... | collective-permute-start | bytes 98312 | tf_op jit(solution)/shard_map/ppermute | solution.py:22
  132.6 4.7 collective-permute-start.8
  137.9 8.6 %collective-permute-start.11 = (f32[2,1,32,128]{3,2,1,0:T(8,128)S(1)}, f32[2,1,32,128]{3,2,1,0:T(8,128)S(1)}, u32[]{:S(2)}, u32[]{:S(2)}) collective-permute-start(f32[2,1,32,128]{3,2,1,0:T(8,128)S(1)} %pad_maximum_fusion.68), channel_id=1, source_target_pairs={{0,16},{16,32},{32,48},{48,64},{64,80},{80,96},{96,112},{1,17},{17... | collective-permute-start | bytes 98312 | tf_op jit(solution)/shard_map/ppermute | solution.py:22
  140.7 6.7 %collective-permute-start.10 = (f32[2,32,1,128]{3,1,2,0:T(8,128)S(1)}, f32[2,32,1,128]{3,1,2,0:T(8,128)S(1)}, u32[]{:S(2)}, u32[]{:S(2)}) collective-permute-start(f32[2,32,1,128]{3,1,2,0:T(8,128)S(1)} %pad_maximum_fusion.67), channel_id=1, source_target_pairs={{0,1},{1,2},{2,3},{3,4},{4,5},{5,6},{6,7},{7,8},{8,9},{9,10},{10,1... | collective-permute-start | bytes 98312 | tf_op jit(solution)/shard_map/ppermute | solution.py:22
  148.8 5.8 %collective-permute-start.13 = (f32[2,32,1,128]{3,1,2,0:T(8,128)S(1)}, f32[2,32,1,128]{3,1,2,0:T(8,128)S(1)}, u32[]{:S(2)}, u32[]{:S(2)}) collective-permute-start(f32[2,32,1,128]{3,1,2,0:T(8,128)S(1)} %pad_maximum_fusion.70), channel_id=1, source_target_pairs={{1,0},{2,1},{3,2},{4,3},{5,4},{6,5},{7,6},{8,7},{9,8},{10,9},{11,1... | collective-permute-start | bytes 98312 | tf_op jit(solution)/shard_map/ppermute | solution.py:22
  150.7 4.7 collective-permute-start.12
  155.9 10.6 %copy-start.2 = (f32[32,32,128]{2,1,0:T(8,128)}, f32[32,32,128]{2,1,0:T(8,128)S(1)}, u32[]{:S(2)}) copy-start(f32[32,32,128]{2,1,0:T(8,128)S(1)} %get-tuple-element.171) | copy-start | bytes 1572868
  155.9 10.6 %copy-start.12 = (f32[32,32,128]{2,1,0:T(8,128)}, f32[32,32,128]{2,1,0:T(8,128)S(1)}, u32[]{:S(2)}) copy-start(f32[32,32,128]{2,1,0:T(8,128)S(1)} %get-tuple-element.170) | copy-start | bytes 1572868
  156.0 10.6 %copy-start.14 = (f32[32,32,128]{2,1,0:T(8,128)}, f32[32,32,128]{2,1,0:T(8,128)S(1)}, u32[]{:S(2)}) copy-start(f32[32,32,128]{2,1,0:T(8,128)S(1)} %get-tuple-element.169) | copy-start | bytes 1572868
  156.1 8.5 %collective-permute-start.14 = (f32[2,32,1,128]{3,1,2,0:T(8,128)S(1)}, f32[2,32,1,128]{3,1,2,0:T(8,128)S(1)}, u32[]{:S(2)}, u32[]{:S(2)}) collective-permute-start(f32[2,32,1,128]{3,1,2,0:T(8,128)S(1)} %pad_maximum_fusion.71), channel_id=1, source_target_pairs={{0,1},{1,2},{2,3},{3,4},{4,5},{5,6},{6,7},{7,8},{8,9},{9,10},{10,1... | collective-permute-start | bytes 98312 | tf_op jit(solution)/shard_map/ppermute | solution.py:22
  161.5 4.1 collective-permute-start.15
  173.1 157.1 %copy-start.37 = (f32[256,256]{1,0:T(8,128)S(1)}, f32[256,256]{1,0:T(8,128)}, u32[]{:S(2)}) copy-start(f32[256,256]{1,0:T(8,128)} %param.25) | copy-start | bytes 786436
  341.5 14.9 %copy-start.48 = (f32[1,32,1,128]{3,1,2,0:T(8,128)S(1)}, f32[1,32,1,128]{3,1,2,0:T(8,128)}, u32[]{:S(2)}) copy-start(f32[1,32,1,128]{3,1,2,0:T(8,128)} %copy-done.47) | copy-start | bytes 49156
  344.5 11.8 %collective-permute-start.21 = (f32[2,32,1,128]{3,1,2,0:T(8,128)S(1)}, f32[2,32,1,128]{3,1,2,0:T(8,128)S(1)}, u32[]{:S(2)}, u32[]{:S(2)}) collective-permute-start(f32[2,32,1,128]{3,1,2,0:T(8,128)S(1)} %pad_maximum_fusion.80), channel_id=1, source_target_pairs={{1,0},{2,1},{3,2},{4,3},{5,4},{6,5},{7,6},{8,7},{9,8},{10,9},{11,1... | collective-permute-start | bytes 98312 | tf_op jit(solution)/shard_map/ppermute | solution.py:22
  347.1 9.2 %collective-permute-start.20 = (f32[2,1,32,128]{3,2,1,0:T(8,128)}, f32[2,1,32,128]{3,2,1,0:T(8,128)S(1)}, u32[]{:S(2)}, u32[]{:S(2)}) collective-permute-start(f32[2,1,32,128]{3,2,1,0:T(8,128)} %pad_maximum_fusion.79), channel_id=1, source_target_pairs={{16,0},{32,16},{48,32},{64,48},{80,64},{96,80},{112,96},{17,1},{33... | collective-permute-start | bytes 98312 | tf_op jit(solution)/shard_map/ppermute | solution.py:22
  356.3 13.4 %copy-start.7 = (f32[32,32,128]{2,1,0:T(8,128)S(1)}, f32[32,32,128]{2,1,0:T(8,128)}, u32[]{:S(2)}) copy-start(f32[32,32,128]{2,1,0:T(8,128)} %copy-done.6) | copy-start | bytes 1572868
  356.3 13.4 %copy-start.17 = (f32[32,32,128]{2,1,0:T(8,128)S(1)}, f32[32,32,128]{2,1,0:T(8,128)}, u32[]{:S(2)}) copy-start(f32[32,32,128]{2,1,0:T(8,128)} %copy-done.16) | copy-start | bytes 1572868
  356.3 13.4 %copy-start.19 = (f32[32,32,128]{2,1,0:T(8,128)S(1)}, f32[32,32,128]{2,1,0:T(8,128)}, u32[]{:S(2)}) copy-start(f32[32,32,128]{2,1,0:T(8,128)} %copy-done.18) | copy-start | bytes 1572868
  356.3 13.4 %copy-start.41 = (f32[32,32,1]{2,1,0:T(8,128)S(1)}, f32[32,32,1]{2,1,0:T(8,128)}, u32[]{:S(2)}) copy-start(f32[32,32,1]{2,1,0:T(8,128)} %copy.4994) | copy-start | bytes 12292
  356.3 13.5 %copy-start.42 = (f32[32,32,1]{2,1,0:T(8,128)S(1)}, f32[32,32,1]{2,1,0:T(8,128)}, u32[]{:S(2)}) copy-start(f32[32,32,1]{2,1,0:T(8,128)} %copy.4992) | copy-start | bytes 12292
  360.5 8.2 %collective-permute-start.23 = (f32[2,1,32,128]{3,2,1,0:T(8,128)S(1)}, f32[2,1,32,128]{3,2,1,0:T(8,128)S(1)}, u32[]{:S(2)}, u32[]{:S(2)}) collective-permute-start(f32[2,1,32,128]{3,2,1,0:T(8,128)S(1)} %pad_maximum_fusion.82), channel_id=1, source_target_pairs={{0,16},{16,32},{32,48},{48,64},{64,80},{80,96},{96,112},{1,17},{17... | collective-permute-start | bytes 98312 | tf_op jit(solution)/shard_map/ppermute | solution.py:22
  364.5 5.2 %collective-permute-start.22 = (f32[2,32,1,128]{3,1,2,0:T(8,128)S(1)}, f32[2,32,1,128]{3,1,2,0:T(8,128)S(1)}, u32[]{:S(2)}, u32[]{:S(2)}) collective-permute-start(f32[2,32,1,128]{3,1,2,0:T(8,128)S(1)} %pad_maximum_fusion.81), channel_id=1, source_target_pairs={{0,1},{1,2},{2,3},{3,4},{4,5},{5,6},{6,7},{7,8},{8,9},{9,10},{10,1... | collective-permute-start | bytes 98312 | tf_op jit(solution)/shard_map/ppermute | solution.py:22
  370.6 18.2 %copy-start.39 = (f32[32,32,1]{2,1,0:T(8,128)S(1)}, f32[32,32,1]{2,1,0:T(8,128)}, u32[]{:S(2)}) copy-start(f32[32,32,1]{2,1,0:T(8,128)} %copy.5002) | copy-start | bytes 12292
  370.6 18.2 %copy-start.40 = (f32[32,32,1]{2,1,0:T(8,128)S(1)}, f32[32,32,1]{2,1,0:T(8,128)}, u32[]{:S(2)}) copy-start(f32[32,32,1]{2,1,0:T(8,128)} %copy.5000) | copy-start | bytes 12292
  370.7 5.9 %collective-permute-start.25 = (f32[2,32,1,128]{3,1,2,0:T(8,128)S(1)}, f32[2,32,1,128]{3,1,2,0:T(8,128)S(1)}, u32[]{:S(2)}, u32[]{:S(2)}) collective-permute-start(f32[2,32,1,128]{3,1,2,0:T(8,128)S(1)} %pad_maximum_fusion.84), channel_id=1, source_target_pairs={{1,0},{2,1},{3,2},{4,3},{5,4},{6,5},{7,6},{8,7},{9,8},{10,9},{11,1... | collective-permute-start | bytes 98312 | tf_op jit(solution)/shard_map/ppermute | solution.py:22
  372.8 4.7 collective-permute-start.24
  378.1 9.7 %collective-permute-start.27 = (f32[2,1,32,128]{3,2,1,0:T(8,128)S(1)}, f32[2,1,32,128]{3,2,1,0:T(8,128)S(1)}, u32[]{:S(2)}, u32[]{:S(2)}) collective-permute-start(f32[2,1,32,128]{3,2,1,0:T(8,128)S(1)} %pad_maximum_fusion.86), channel_id=1, source_target_pairs={{0,16},{16,32},{32,48},{48,64},{64,80},{80,96},{96,112},{1,17},{17... | collective-permute-start | bytes 98312 | tf_op jit(solution)/shard_map/ppermute | solution.py:22
  382.2 6.7 %collective-permute-start.26 = (f32[2,32,1,128]{3,1,2,0:T(8,128)S(1)}, f32[2,32,1,128]{3,1,2,0:T(8,128)S(1)}, u32[]{:S(2)}, u32[]{:S(2)}) collective-permute-start(f32[2,32,1,128]{3,1,2,0:T(8,128)S(1)} %pad_maximum_fusion.85), channel_id=1, source_target_pairs={{0,1},{1,2},{2,3},{3,4},{4,5},{5,6},{6,7},{7,8},{8,9},{9,10},{10,1... | collective-permute-start | bytes 98312 | tf_op jit(solution)/shard_map/ppermute | solution.py:22
  389.8 5.8 %collective-permute-start.29 = (f32[2,32,1,128]{3,1,2,0:T(8,128)S(1)}, f32[2,32,1,128]{3,1,2,0:T(8,128)S(1)}, u32[]{:S(2)}, u32[]{:S(2)}) collective-permute-start(f32[2,32,1,128]{3,1,2,0:T(8,128)S(1)} %pad_maximum_fusion.88), channel_id=1, source_target_pairs={{1,0},{2,1},{3,2},{4,3},{5,4},{6,5},{7,6},{8,7},{9,8},{10,9},{11,1... | collective-permute-start | bytes 98312 | tf_op jit(solution)/shard_map/ppermute | solution.py:22
  391.7 4.7 collective-permute-start.28
  396.4 10.6 %copy-start.9 = (f32[32,32,128]{2,1,0:T(8,128)S(1)}, f32[32,32,128]{2,1,0:T(8,128)}, u32[]{:S(2)}) copy-start(f32[32,32,128]{2,1,0:T(8,128)} %copy-done.8) | copy-start | bytes 1572868
  396.4 10.6 %copy-start.11 = (f32[32,32,128]{2,1,0:T(8,128)S(1)}, f32[32,32,128]{2,1,0:T(8,128)}, u32[]{:S(2)}) copy-start(f32[32,32,128]{2,1,0:T(8,128)} %copy-done.10) | copy-start | bytes 1572868
  396.4 10.6 %copy-start.26 = (f32[32,32,128]{2,1,0:T(8,128)S(1)}, f32[32,32,128]{2,1,0:T(8,128)}, u32[]{:S(2)}) copy-start(f32[32,32,128]{2,1,0:T(8,128)} %copy-done.24) | copy-start | bytes 1572868
  396.4 10.6 %copy-start.29 = (f32[32,32,128]{2,1,0:T(8,128)S(1)}, f32[32,32,128]{2,1,0:T(8,128)}, u32[]{:S(2)}) copy-start(f32[32,32,128]{2,1,0:T(8,128)} %copy-done.27) | copy-start | bytes 1572868
  396.4 10.6 %copy-start.32 = (f32[32,32,128]{2,1,0:T(8,128)S(1)}, f32[32,32,128]{2,1,0:T(8,128)}, u32[]{:S(2)}) copy-start(f32[32,32,128]{2,1,0:T(8,128)} %get-tuple-element.143) | copy-start | bytes 1572868
  397.6 8.4 %collective-permute-start.31 = (f32[2,1,32,128]{3,2,1,0:T(8,128)S(1)}, f32[2,1,32,128]{3,2,1,0:T(8,128)S(1)}, u32[]{:S(2)}, u32[]{:S(2)}) collective-permute-start(f32[2,1,32,128]{3,2,1,0:T(8,128)S(1)} %pad_maximum_fusion.90), channel_id=1, source_target_pairs={{0,16},{16,32},{32,48},{48,64},{64,80},{80,96},{96,112},{1,17},{17... | collective-permute-start | bytes 98312 | tf_op jit(solution)/shard_map/ppermute | solution.py:22
  400.3 6.7 %collective-permute-start.30 = (f32[2,32,1,128]{3,1,2,0:T(8,128)S(1)}, f32[2,32,1,128]{3,1,2,0:T(8,128)S(1)}, u32[]{:S(2)}, u32[]{:S(2)}) collective-permute-start(f32[2,32,1,128]{3,1,2,0:T(8,128)S(1)} %pad_maximum_fusion.89), channel_id=1, source_target_pairs={{0,1},{1,2},{2,3},{3,4},{4,5},{5,6},{6,7},{7,8},{8,9},{9,10},{10,1... | collective-permute-start | bytes 98312 | tf_op jit(solution)/shard_map/ppermute | solution.py:22
  412.5 48.3 %copy-start.3 = (f32[32,32,128]{2,1,0:T(8,128)S(1)}, f32[32,32,128]{2,1,0:T(8,128)}, u32[]{:S(2)}) copy-start(f32[32,32,128]{2,1,0:T(8,128)} %copy-done.2) | copy-start | bytes 1572868
  441.0 30.0 %all-to-all-start.2 = ((f32[128,2,16]{2,1,0:T(2,128)}), f32[128,2,16]{2,1,0:T(2,128)S(1)}, u32[]{:S(2)}, u32[]{:S(2)}) async-start(f32[128,2,16]{2,1,0:T(2,128)} %reshape.462), calls=%async_computation.2 | async-start | bytes 262144 | tf_op jit(solution)/shard_map/all_to_all | solution.py:194
  (27 other events, 186.5 us)
Sparse Core Ops, SparseCore 0:
  173.2 156.9 all-reduce.44
where the time goes:
time: 481 us; the launch traced here: 479 us
  waiting for transfers between devices  189 us (39%)
  starting transfers between devices  135 us (28%)
  local copies, waits for them, and re-layouts  63.3 us (13%)
  other arithmetic  62.6 us (13%)
  between operations  16.2 us (3%)
  matrix products  13.1 us (3%)
    psum x1, waiting for transfers between devices, shards(): far_field = lax.psum(partial_far, ('gx', 'gy'))  152 us
    ppermute x32, starting transfers between devices, passed_along(): return lax.ppermute(shard, axis, pairs)  91.1 us
    unnamed x7, other arithmetic  33.4 us
    gather x1, local copies, waits for them, and re-layouts, shards(): picked = column_grad[cells_x, cells_y]  27.6 us
    ppermute x32, waiting for transfers between devices, passed_along(): return lax.ppermute(shard, axis, pairs)  21.6 us
    all_to_all x1, starting transfers between devices, shards(): lax.all_to_all(picked.reshape(devices, capacity, 16), ('gx', 'gy'), split...  19.8 us
    dot_general x16, matrix products, contract(): jnp.einsum(pattern, first_op, second_op, precision=lax.Precision.HIGHEST)  13.1 us
    all_to_all x1, starting transfers between devices, shards(): lax.all_to_all(packed_at.reshape(devices, capacity, 2), ('gx', 'gy'), spl...  12.4 us
  transfers between devices with their start and end apart: 36, of which 19 were waited for; matrix products, arithmetic and copies ran while one was open for 14% of the time, Pallas kernels for 0%

commit v1 on v0

--- a/solution.py
+++ b/solution.py
@@ -165,7 +165,7 @@
     row_count = U // devices
     row_start = linear * row_count
     partial_far = project_forward(mon_re, mon_im, table_x, table_y, norm_scale)
-    far_field = lax.psum(partial_far, ("gx", "gy"))
+    far_field = lax.psum(lax.psum(partial_far, "gx"), "gy")
     mine_rows = lax.dynamic_slice_in_dim(far_field, row_start, row_count, 2)
     focal_power = jnp.sum(mine_rows * mine_rows, axis=(0, 1))
     weighted = jnp.stack([target * far_field[0], -(target * far_field[1])])

time: 481 us -> 555 us (1.15)
  waiting for transfers between devices: 189 us -> 262 us
    psum x1 -> x2, waiting for transfers between devices: 152 us -> 224 us  [shards(): far_field = lax.psum(lax.psum(partial_far, 'gx'), 'gy')]
  transfers between devices with their start and end apart: 36 -> 37, of which waited for: 19 -> 21; matrix products, arithmetic and copies ran while one was open for 14% -> 12% of each run, Pallas kernels for 0% -> 0%
where the time goes in v1:
time: 555 us; the launch traced here: 554 us
  waiting for transfers between devices  262 us (47%)
  starting transfers between devices  138 us (25%)
  local copies, waits for them, and re-layouts  62.7 us (11%)
  other arithmetic  61.4 us (11%)
  between operations  16.4 us (3%)
  matrix products  13.1 us (2%)
    psum x2, waiting for transfers between devices, shards(): far_field = lax.psum(lax.psum(partial_far, 'gx'), 'gy')  224 us
    ppermute x32, starting transfers between devices, passed_along(): return lax.ppermute(shard, axis, pairs)  91.6 us
    unnamed x7, other arithmetic  32.5 us
    gather x1, local copies, waits for them, and re-layouts, shards(): picked = column_grad[cells_x, cells_y]  27.6 us
    all_to_all x1, starting transfers between devices, shards(): lax.all_to_all(picked.reshape(devices, capacity, 16), ('gx', 'gy'), split...  22.3 us
    ppermute x32, waiting for transfers between devices, passed_along(): return lax.ppermute(shard, axis, pairs)  21.3 us
    dot_general x16, matrix products, contract(): jnp.einsum(pattern, first_op, second_op, precision=lax.Precision.HIGHEST)  13.1 us
    all_to_all x1, starting transfers between devices, shards(): lax.all_to_all(packed_at.reshape(devices, capacity, 2), ('gx', 'gy'), spl...  12.4 us
  transfers between devices with their start and end apart: 37, of which 21 were waited for; matrix products, arithmetic and copies ran while one was open for 12% of the time, Pallas kernels for 0%

profile of v1, /device:TPU:1, one launch (start us, length us, event | category | flops | bytes accessed | tf_op | source)
XLA Modules:
  0.0 553.7 jit_solution(7364321585917053926)
XLA Ops:
  7.8 1.4 collective-permute-start.16
  9.9 3.3 collective-permute-start.17
  17.3 1.5 copy.4958
  18.8 12.4 %all-to-all-start = ((f32[128,2,2]{1,2,0:T(2,128)}), f32[128,2,2]{1,2,0:T(2,128)S(1)}, u32[]{:S(2)}, u32[]{:S(2)}) async-start(f32[128,2,2]{1,2,0:T(2,128)} %copy.4958), calls=%async_computation | async-start | bytes 262144 | tf_op jit(solution)/shard_map/all_to_all | solution.py:126
  31.2 2.3 slice_bitcast_fusion.3
  35.1 3.0 collective-permute-start.1
  38.1 1.3 collective-permute-start
  39.7 1.5 scatter_custom_fusion.1
  41.4 11.3 %all-to-all-start.1 = ((f32[128,2,16]{2,1,0:T(2,128)}), f32[128,2,16]{2,1,0:T(2,128)S(1)}, u32[]{:S(2)}, u32[]{:S(2)}) async-start(f32[128,2,16]{2,1,0:T(2,128)} %bitcast.24), calls=%async_computation.1 | async-start | bytes 262144 | tf_op jit(solution)/shard_map/all_to_all | solution.py:119
  54.1 8.7 %all-to-all-done.1 = f32[128,2,16]{2,1,0:T(2,128)S(1)} async-done(((f32[128,2,16]{2,1,0:T(2,128)}), f32[128,2,16]{2,1,0:T(2,128)S(1)}, u32[]{:S(2)}, u32[]{:S(2)}) %all-to-all-start.1) | async-done | bytes 16416 | tf_op jit(solution)/shard_map/all_to_all | solution.py:119
  63.0 28.8 %scatter_custom_fusion.2 = f32[1024]{0:T(1024)S(1)} fusion(s32[4096]{0:T(1024)S(1)} %reshape.500, f32[4096]{0:T(1024)S(1)} %reshape.502, f32[]{:T(128)} %constant.251.clone.1), kind=kCustom, calls=%fused_computation.635 | custom fusion | flops 4096 | bytes 4100
  94.1 2.7 collective-permute-start.18
  96.8 2.2 collective-permute-start.19
  99.8 3.5 collective-permute-start.3
  103.3 2.6 collective-permute-start.2
  109.7 1.9 collective-permute-start.5
  111.6 1.3 collective-permute-start.4
  112.9 2.0 collective-permute-done.5
  114.9 1.4 collective-permute-done.4
  116.9 3.1 collective-permute-start.7
  120.1 5.1 collective-permute-start.6
  127.6 1.9 collective-permute-start.9
  129.6 1.3 collective-permute-start.8
  130.9 2.6 collective-permute-done.9
  134.8 2.7 collective-permute-start.11
  137.6 5.8 %collective-permute-start.10 = (f32[2,32,1,128]{3,1,2,0:T(8,128)S(1)}, f32[2,32,1,128]{3,1,2,0:T(8,128)S(1)}, u32[]{:S(2)}, u32[]{:S(2)}) collective-permute-start(f32[2,32,1,128]{3,1,2,0:T(8,128)S(1)} %pad_maximum_fusion.67), channel_id=1, source_target_pairs={{0,1},{1,2},{2,3},{3,4},{4,5},{5,6},{6,7},{7,8},{8,9},{9,10},{10,1... | collective-permute-start | bytes 98312 | tf_op jit(solution)/shard_map/ppermute | solution.py:22
  145.7 1.9 collective-permute-start.13
  147.7 1.3 collective-permute-start.12
  149.0 2.6 collective-permute-done.13
  153.0 5.4 collective-permute-start.14
  158.4 3.1 collective-permute-start.15
  170.4 86.0 %all-reduce.46.cloned.1.call-done = f32[2,2,256,256]{3,2,1,0:T(8,128)} async-done(((f32[2,2,256,256]{3,2,1,0:T(8,128)}), f32[2,2,256,256]{3,2,1,0:T(8,128)}) %all-reduce.46.cloned.1.call-update) | async-done | bytes 1048592 | tf_op jit(solution)/shard_map/psum | solution.py:168
  259.7 3.1 bitcast_dynamic-update-slice_fusion.3
  264.4 138.1 %all-reduce.48.cloned.1.call-done = f32[2,2,256,256]{3,2,1,0:T(8,128)} async-done(((f32[2,2,256,256]{3,2,1,0:T(8,128)}), f32[2,2,256,256]{3,2,1,0:T(8,128)}) %all-reduce.48.cloned.1.call-update) | async-done | bytes 1048592 | tf_op jit(solution)/shard_map/psum | solution.py:168
  402.5 1.8 fusion.284
  404.3 1.8 convolution_add_fusion.2
  406.5 1.8 fusion.286
  408.3 1.8 convolution_subtract_fusion.2
  411.3 1.3 copy.4986
  413.8 3.0 fusion.94
  416.8 2.8 collective-permute-start.21
  419.6 1.3 collective-permute-start.20
  421.0 1.3 copy.4994
  422.3 1.3 copy.4992
  423.6 1.3 copy.5002
  424.9 1.3 copy.5000
  428.8 3.9 fusion.98
  432.8 4.0 collective-permute-start.23
  436.8 3.4 collective-permute-start.22
  442.2 2.1 collective-permute-start.25
  444.3 1.3 collective-permute-start.24
  445.6 2.6 collective-permute-done.25
  449.6 4.0 collective-permute-start.27
  453.6 5.7 %collective-permute-start.26 = (f32[2,32,1,128]{3,1,2,0:T(8,128)S(1)}, f32[2,32,1,128]{3,1,2,0:T(8,128)S(1)}, u32[]{:S(2)}, u32[]{:S(2)}) collective-permute-start(f32[2,32,1,128]{3,1,2,0:T(8,128)S(1)} %pad_maximum_fusion.85), channel_id=1, source_target_pairs={{0,1},{1,2},{2,3},{3,4},{4,5},{5,6},{6,7},{7,8},{8,9},{9,10},{10,1... | collective-permute-start | bytes 98312 | tf_op jit(solution)/shard_map/ppermute | solution.py:22
  461.2 1.9 collective-permute-start.29
  463.1 1.6 collective-permute-start.28
  464.7 2.3 collective-permute-done.29
  469.0 3.3 collective-permute-start.31
  472.3 5.7 %collective-permute-start.30 = (f32[2,32,1,128]{3,1,2,0:T(8,128)S(1)}, f32[2,32,1,128]{3,1,2,0:T(8,128)S(1)}, u32[]{:S(2)}, u32[]{:S(2)}) collective-permute-start(f32[2,32,1,128]{3,1,2,0:T(8,128)S(1)} %pad_maximum_fusion.89), channel_id=1, source_target_pairs={{0,1},{1,2},{2,3},{3,4},{4,5},{5,6},{6,7},{7,8},{8,9},{9,10},{10,1... | collective-permute-start | bytes 98312 | tf_op jit(solution)/shard_map/ppermute | solution.py:22
  479.1 5.4 fusion.147
  484.6 27.6 %gather_fusion = f32[4096]{0:T(1024)S(1)} fusion(f32[32,32]{0,1:T(8,128)S(1)} %copy.5037, s32[4096]{0:T(1024)S(1)} %reshape.470), kind=kCustom, calls=%fused_computation | custom fusion | bytes 65536 | tf_op jit(solution)/shard_map/gather | solution.py:193
  513.0 22.3 %all-to-all-start.2 = ((f32[128,2,16]{2,1,0:T(2,128)}), f32[128,2,16]{2,1,0:T(2,128)S(1)}, u32[]{:S(2)}, u32[]{:S(2)}) async-start(f32[128,2,16]{2,1,0:T(2,128)} %reshape.462), calls=%async_computation.2 | async-start | bytes 262144 | tf_op jit(solution)/shard_map/all_to_all | solution.py:194
  536.2 1.4 multiply_reduce_fusion.2
  537.5 7.9 %all-to-all-done.2 = f32[128,2,16]{2,1,0:T(2,128)S(1)} async-done(((f32[128,2,16]{2,1,0:T(2,128)}), f32[128,2,16]{2,1,0:T(2,128)S(1)}, u32[]{:S(2)}, u32[]{:S(2)}) %all-to-all-start.2) | async-done | bytes 16416 | tf_op jit(solution)/shard_map/all_to_all | solution.py:194
  (379 shorter events, 53.7 us)
Async XLA Ops:
  7.2 46.6 %copy-start.66 = (s32[2]{0:T(128)S(1)}, s32[2]{0:T(128)}, u32[]{:S(2)}) copy-start(s32[2]{0:T(128)} %constant.375) | copy-start | bytes 28
  7.2 30.9 %copy-start.19 = (f32[6,32,32,128]{3,2,1,0:T(8,128)S(1)}, f32[6,32,32,128]{3,2,1,0:T(8,128)}, u32[]{:S(2)}) copy-start(f32[6,32,32,128]{3,2,1,0:T(8,128)} %param.23) | copy-start | bytes 9437188
  7.2 32.3 %copy-start.63 = (f32[128,16]{0,1:T(8,128)S(1)}, f32[128,16]{0,1:T(8,128)}, u32[]{:S(2)}) copy-start(f32[128,16]{0,1:T(8,128)} %param.27) | copy-start | bytes 24580
  7.2 32.3 %copy-start.67 = (f32[128]{0:T(128)S(1)}, f32[128]{0:T(128)}, u32[]{:S(2)}) copy-start(f32[128]{0:T(128)} %param.26) | copy-start | bytes 1540
  7.8 84.0 %collective-permute-start.16 = (f32[2,1,32,128]{3,2,1,0:T(8,128)}, f32[2,1,32,128]{3,2,1,0:T(8,128)}, u32[]{:S(2)}, u32[]{:S(2)}) collective-permute-start(f32[2,1,32,128]{3,2,1,0:T(8,128)} %stack.374), channel_id=1, source_target_pairs={{16,0},{32,16},{48,32},{64,48},{80,64},{96,80},{112,96},{17,1},{33... | collective-permute-start | bytes 98312 | tf_op jit(solution)/shard_map/ppermute | solution.py:22
  9.9 82.9 %collective-permute-start.17 = (f32[2,32,1,128]{3,1,2,0:T(8,128)}, f32[2,32,1,128]{3,1,2,0:T(8,128)}, u32[]{:S(2)}, u32[]{:S(2)}) collective-permute-start(f32[2,32,1,128]{3,1,2,0:T(8,128)} %stack.375), channel_id=1, source_target_pairs={{1,0},{2,1},{3,2},{4,3},{5,4},{6,5},{7,6},{8,7},{9,8},{10,9},{11,1... | collective-permute-start | bytes 98312 | tf_op jit(solution)/shard_map/ppermute | solution.py:22
  15.6 25.8 %copy-start.68 = (s32[128]{0:T(128)}, s32[128]{0:T(128)S(1)}, u32[]{:S(2)}) copy-start(s32[128]{0:T(128)S(1)} %fusion.391) | copy-start | bytes 1540
  18.8 22.5 %all-to-all-start = ((f32[128,2,2]{1,2,0:T(2,128)}), f32[128,2,2]{1,2,0:T(2,128)S(1)}, u32[]{:S(2)}, u32[]{:S(2)}) async-start(f32[128,2,2]{1,2,0:T(2,128)} %copy.4958), calls=%async_computation | async-start | bytes 262144 | tf_op jit(solution)/shard_map/all_to_all | solution.py:126
  35.1 63.9 %collective-permute-start.1 = (f32[2,32,1,128]{3,1,2,0:T(8,128)}, f32[2,32,1,128]{3,1,2,0:T(8,128)S(1)}, u32[]{:S(2)}, u32[]{:S(2)}) collective-permute-start(f32[2,32,1,128]{3,1,2,0:T(8,128)} %pad_maximum_fusion.58), channel_id=1, source_target_pairs={{1,0},{2,1},{3,2},{4,3},{5,4},{6,5},{7,6},{8,7},{9,8},{10,9},{11,1... | collective-permute-start | bytes 98312 | tf_op jit(solution)/shard_map/ppermute | solution.py:22
  38.1 60.9 %collective-permute-start = (f32[2,1,32,128]{3,2,1,0:T(8,128)S(1)}, f32[2,1,32,128]{3,2,1,0:T(8,128)S(1)}, u32[]{:S(2)}, u32[]{:S(2)}) collective-permute-start(f32[2,1,32,128]{3,2,1,0:T(8,128)S(1)} %stack.314), channel_id=1, source_target_pairs={{16,0},{32,16},{48,32},{64,48},{80,64},{96,80},{112,96},{17,1},{33... | collective-permute-start | bytes 98312 | tf_op jit(solution)/shard_map/ppermute | solution.py:22
  39.5 128.7 %copy-start.47 = (f32[256]{0:T(256)}, f32[256]{0:T(256)S(1)}, u32[]{:S(2)}) copy-start(f32[256]{0:T(256)S(1)} %multiply_add_fusion.1) | copy-start | bytes 3076
  39.5 127.5 %copy-start.61 = (f32[32]{0:T(128)}, f32[32]{0:T(128)S(1)}, u32[]{:S(2)}) copy-start(f32[32]{0:T(128)S(1)} %multiply_add_fusion.3) | copy-start | bytes 388
  39.6 128.6 %copy-start.64 = (f32[32]{0:T(128)}, f32[32]{0:T(128)S(1)}, u32[]{:S(2)}) copy-start(f32[32]{0:T(128)S(1)} %multiply_add_fusion.2) | copy-start | bytes 388
  41.4 21.4 %all-to-all-start.1 = ((f32[128,2,16]{2,1,0:T(2,128)}), f32[128,2,16]{2,1,0:T(2,128)S(1)}, u32[]{:S(2)}, u32[]{:S(2)}) async-start(f32[128,2,16]{2,1,0:T(2,128)} %bitcast.24), calls=%async_computation.1 | async-start | bytes 262144 | tf_op jit(solution)/shard_map/all_to_all | solution.py:119
  52.7 203.7 %all-reduce.46.cloned.1.call-start = ((), (), s32[]{:S(2)}) async-start(), calls=%async_computation.3 | async-start | bytes 2097152 | tf_op jit(solution)/shard_map/psum | solution.py:168
  94.1 11.9 %collective-permute-start.18 = (f32[2,32,1,128]{3,1,2,0:T(8,128)S(1)}, f32[2,32,1,128]{3,1,2,0:T(8,128)S(1)}, u32[]{:S(2)}, u32[]{:S(2)}) collective-permute-start(f32[2,32,1,128]{3,1,2,0:T(8,128)S(1)} %pad_maximum_fusion.77), channel_id=1, source_target_pairs={{0,1},{1,2},{2,3},{3,4},{4,5},{5,6},{6,7},{7,8},{8,9},{9,10},{10,1... | collective-permute-start | bytes 98312 | tf_op jit(solution)/shard_map/ppermute | solution.py:22
  96.8 9.8 %collective-permute-start.19 = (f32[2,1,32,128]{3,2,1,0:T(8,128)S(1)}, f32[2,1,32,128]{3,2,1,0:T(8,128)S(1)}, u32[]{:S(2)}, u32[]{:S(2)}) collective-permute-start(f32[2,1,32,128]{3,2,1,0:T(8,128)S(1)} %pad_maximum_fusion.78), channel_id=1, source_target_pairs={{0,16},{16,32},{32,48},{48,64},{64,80},{80,96},{96,112},{1,17},{17... | collective-permute-start | bytes 98312 | tf_op jit(solution)/shard_map/ppermute | solution.py:22
  99.8 8.4 %collective-permute-start.3 = (f32[2,1,32,128]{3,2,1,0:T(8,128)S(1)}, f32[2,1,32,128]{3,2,1,0:T(8,128)S(1)}, u32[]{:S(2)}, u32[]{:S(2)}) collective-permute-start(f32[2,1,32,128]{3,2,1,0:T(8,128)S(1)} %pad_maximum_fusion.60), channel_id=1, source_target_pairs={{0,16},{16,32},{32,48},{48,64},{64,80},{80,96},{96,112},{1,17},{17... | collective-permute-start | bytes 98312 | tf_op jit(solution)/shard_map/ppermute | solution.py:22
  103.3 4.9 collective-permute-start.2
  108.8 17.3 %copy-start.7 = (f32[32,32,128]{2,1,0:T(8,128)}, f32[32,32,128]{2,1,0:T(8,128)S(1)}, u32[]{:S(2)}) copy-start(f32[32,32,128]{2,1,0:T(8,128)S(1)} %get-tuple-element.138) | copy-start | bytes 1572868
  109.7 5.2 collective-permute-start.5
  111.6 4.7 collective-permute-start.4
  116.9 8.2 %collective-permute-start.7 = (f32[2,1,32,128]{3,2,1,0:T(8,128)S(1)}, f32[2,1,32,128]{3,2,1,0:T(8,128)S(1)}, u32[]{:S(2)}, u32[]{:S(2)}) collective-permute-start(f32[2,1,32,128]{3,2,1,0:T(8,128)S(1)} %pad_maximum_fusion.64), channel_id=1, source_target_pairs={{0,16},{16,32},{32,48},{48,64},{64,80},{80,96},{96,112},{1,17},{17... | collective-permute-start | bytes 98312 | tf_op jit(solution)/shard_map/ppermute | solution.py:22
  120.1 6.1 %collective-permute-start.6 = (f32[2,32,1,128]{3,1,2,0:T(8,128)S(1)}, f32[2,32,1,128]{3,1,2,0:T(8,128)S(1)}, u32[]{:S(2)}, u32[]{:S(2)}) collective-permute-start(f32[2,32,1,128]{3,1,2,0:T(8,128)S(1)} %pad_maximum_fusion.63), channel_id=1, source_target_pairs={{0,1},{1,2},{2,3},{3,4},{4,5},{5,6},{6,7},{7,8},{8,9},{9,10},{10,1... | collective-permute-start | bytes 98312 | tf_op jit(solution)/shard_map/ppermute | solution.py:22
  126.8 17.5 %copy-start = (f32[32,32,128]{2,1,0:T(8,128)}, f32[32,32,128]{2,1,0:T(8,128)S(1)}, u32[]{:S(2)}) copy-start(f32[32,32,128]{2,1,0:T(8,128)S(1)} %get-tuple-element.162) | copy-start | bytes 1572868
  126.8 17.5 %copy-start.9 = (f32[32,32,128]{2,1,0:T(8,128)}, f32[32,32,128]{2,1,0:T(8,128)S(1)}, u32[]{:S(2)}) copy-start(f32[32,32,128]{2,1,0:T(8,128)S(1)} %get-tuple-element.161) | copy-start | bytes 1572868
  127.6 5.8 %collective-permute-start.9 = (f32[2,32,1,128]{3,1,2,0:T(8,128)S(1)}, f32[2,32,1,128]{3,1,2,0:T(8,128)S(1)}, u32[]{:S(2)}, u32[]{:S(2)}) collective-permute-start(f32[2,32,1,128]{3,1,2,0:T(8,128)S(1)} %pad_maximum_fusion.66), channel_id=1, source_target_pairs={{1,0},{2,1},{3,2},{4,3},{5,4},{6,5},{7,6},{8,7},{9,8},{10,9},{11,1... | collective-permute-start | bytes 98312 | tf_op jit(solution)/shard_map/ppermute | solution.py:22
  129.6 4.7 collective-permute-start.8
  134.8 8.6 %collective-permute-start.11 = (f32[2,1,32,128]{3,2,1,0:T(8,128)S(1)}, f32[2,1,32,128]{3,2,1,0:T(8,128)S(1)}, u32[]{:S(2)}, u32[]{:S(2)}) collective-permute-start(f32[2,1,32,128]{3,2,1,0:T(8,128)S(1)} %pad_maximum_fusion.68), channel_id=1, source_target_pairs={{0,16},{16,32},{32,48},{48,64},{64,80},{80,96},{96,112},{1,17},{17... | collective-permute-start | bytes 98312 | tf_op jit(solution)/shard_map/ppermute | solution.py:22
  137.6 6.7 %collective-permute-start.10 = (f32[2,32,1,128]{3,1,2,0:T(8,128)S(1)}, f32[2,32,1,128]{3,1,2,0:T(8,128)S(1)}, u32[]{:S(2)}, u32[]{:S(2)}) collective-permute-start(f32[2,32,1,128]{3,1,2,0:T(8,128)S(1)} %pad_maximum_fusion.67), channel_id=1, source_target_pairs={{0,1},{1,2},{2,3},{3,4},{4,5},{5,6},{6,7},{7,8},{8,9},{9,10},{10,1... | collective-permute-start | bytes 98312 | tf_op jit(solution)/shard_map/ppermute | solution.py:22
  145.7 5.8 %collective-permute-start.13 = (f32[2,32,1,128]{3,1,2,0:T(8,128)S(1)}, f32[2,32,1,128]{3,1,2,0:T(8,128)S(1)}, u32[]{:S(2)}, u32[]{:S(2)}) collective-permute-start(f32[2,32,1,128]{3,1,2,0:T(8,128)S(1)} %pad_maximum_fusion.70), channel_id=1, source_target_pairs={{1,0},{2,1},{3,2},{4,3},{5,4},{6,5},{7,6},{8,7},{9,8},{10,9},{11,1... | collective-permute-start | bytes 98312 | tf_op jit(solution)/shard_map/ppermute | solution.py:22
  147.7 4.7 collective-permute-start.12
  153.0 8.5 %collective-permute-start.14 = (f32[2,32,1,128]{3,1,2,0:T(8,128)S(1)}, f32[2,32,1,128]{3,1,2,0:T(8,128)S(1)}, u32[]{:S(2)}, u32[]{:S(2)}) collective-permute-start(f32[2,32,1,128]{3,1,2,0:T(8,128)S(1)} %pad_maximum_fusion.71), channel_id=1, source_target_pairs={{0,1},{1,2},{2,3},{3,4},{4,5},{5,6},{6,7},{7,8},{8,9},{9,10},{10,1... | collective-permute-start | bytes 98312 | tf_op jit(solution)/shard_map/ppermute | solution.py:22
  158.4 4.1 collective-permute-start.15
  167.4 89.0 %copy-start.69 = (s32[128]{0:T(128)S(1)}, s32[128]{0:T(128)}, u32[]{:S(2)}) copy-start(s32[128]{0:T(128)} %copy-done.68) | copy-start | bytes 1540
  167.4 90.3 %copy-start.60 = (s32[256,16,1]{0,1,2:T(8,128)S(1)}, s32[256,16,1]{0,1,2:T(8,128)}, u32[]{:S(2)}) copy-start(s32[256,16,1]{0,1,2:T(8,128)} %get-tuple-element.260) | copy-start | bytes 49156
  170.1 232.4 %all-reduce.48.cloned.1.call-start = ((), (), s32[]{:S(2)}) async-start(), calls=%async_computation.4 | async-start | bytes 2097152 | tf_op jit(solution)/shard_map/psum | solution.py:168
  256.4 146.2 %copy-start.36 = (f32[256,256]{1,0:T(8,128)S(1)}, f32[256,256]{1,0:T(8,128)}, u32[]{:S(2)}) copy-start(f32[256,256]{1,0:T(8,128)} %param.25) | copy-start | bytes 786436
  257.9 144.6 %copy-start.48 = (f32[256]{0:T(256)S(1)}, f32[256]{0:T(256)}, u32[]{:S(2)}) copy-start(f32[256]{0:T(256)} %copy-done.47) | copy-start | bytes 3076
  257.9 144.6 %copy-start.65 = (f32[32]{0:T(128)S(1)}, f32[32]{0:T(128)}, u32[]{:S(2)}) copy-start(f32[32]{0:T(128)} %copy-done.64) | copy-start | bytes 388
  259.7 146.4 %copy-start.62 = (f32[32]{0:T(128)S(1)}, f32[32]{0:T(128)}, u32[]{:S(2)}) copy-start(f32[32]{0:T(128)} %copy-done.61) | copy-start | bytes 388
  263.6 150.2 %copy-start.58 = (f32[1,32,1,128]{3,1,2,0:T(8,128)S(1)}, f32[1,32,1,128]{3,1,2,0:T(8,128)}, u32[]{:S(2)}) copy-start(f32[1,32,1,128]{3,1,2,0:T(8,128)} %get-tuple-element.220) | copy-start | bytes 49156
  263.6 150.2 %copy-start.59 = (f32[1,32,128]{2,1,0:T(8,128)S(1)}, f32[1,32,128]{2,1,0:T(8,128)}, u32[]{:S(2)}) copy-start(f32[1,32,128]{2,1,0:T(8,128)} %get-tuple-element.218) | copy-start | bytes 49156
  413.8 14.9 %copy-start.50 = (f32[1,32,128]{2,1,0:T(8,128)S(1)}, f32[1,32,128]{2,1,0:T(8,128)}, u32[]{:S(2)}) copy-start(f32[1,32,128]{2,1,0:T(8,128)} %copy-done.49) | copy-start | bytes 49156
  413.8 14.9 %copy-start.52 = (f32[1,32,1,128]{3,1,2,0:T(8,128)S(1)}, f32[1,32,1,128]{3,1,2,0:T(8,128)}, u32[]{:S(2)}) copy-start(f32[1,32,1,128]{3,1,2,0:T(8,128)} %copy-done.51) | copy-start | bytes 49156
  413.8 15.0 %copy-start.54 = (f32[1,32,128]{2,1,0:T(8,128)S(1)}, f32[1,32,128]{2,1,0:T(8,128)}, u32[]{:S(2)}) copy-start(f32[1,32,128]{2,1,0:T(8,128)} %copy-done.53) | copy-start | bytes 49156
  413.8 15.0 %copy-start.56 = (f32[1,32,1,128]{3,1,2,0:T(8,128)S(1)}, f32[1,32,1,128]{3,1,2,0:T(8,128)}, u32[]{:S(2)}) copy-start(f32[1,32,1,128]{3,1,2,0:T(8,128)} %copy-done.55) | copy-start | bytes 49156
  416.8 11.8 %collective-permute-start.21 = (f32[2,32,1,128]{3,1,2,0:T(8,128)S(1)}, f32[2,32,1,128]{3,1,2,0:T(8,128)S(1)}, u32[]{:S(2)}, u32[]{:S(2)}) collective-permute-start(f32[2,32,1,128]{3,1,2,0:T(8,128)S(1)} %pad_maximum_fusion.80), channel_id=1, source_target_pairs={{1,0},{2,1},{3,2},{4,3},{5,4},{6,5},{7,6},{8,7},{9,8},{10,9},{11,1... | collective-permute-start | bytes 98312 | tf_op jit(solution)/shard_map/ppermute | solution.py:22
  419.6 9.1 %collective-permute-start.20 = (f32[2,1,32,128]{3,2,1,0:T(8,128)S(1)}, f32[2,1,32,128]{3,2,1,0:T(8,128)S(1)}, u32[]{:S(2)}, u32[]{:S(2)}) collective-permute-start(f32[2,1,32,128]{3,2,1,0:T(8,128)S(1)} %pad_maximum_fusion.79), channel_id=1, source_target_pairs={{16,0},{32,16},{48,32},{64,48},{80,64},{96,80},{112,96},{17,1},{33... | collective-permute-start | bytes 98312 | tf_op jit(solution)/shard_map/ppermute | solution.py:22
  432.8 7.4 %collective-permute-start.23 = (f32[2,1,32,128]{3,2,1,0:T(8,128)S(1)}, f32[2,1,32,128]{3,2,1,0:T(8,128)S(1)}, u32[]{:S(2)}, u32[]{:S(2)}) collective-permute-start(f32[2,1,32,128]{3,2,1,0:T(8,128)S(1)} %pad_maximum_fusion.82), channel_id=1, source_target_pairs={{0,16},{16,32},{32,48},{48,64},{64,80},{80,96},{96,112},{1,17},{17... | collective-permute-start | bytes 98312 | tf_op jit(solution)/shard_map/ppermute | solution.py:22
  436.8 4.4 collective-permute-start.22
  442.1 18.2 %copy-start.38 = (f32[32,32,1]{2,1,0:T(8,128)S(1)}, f32[32,32,1]{2,1,0:T(8,128)}, u32[]{:S(2)}) copy-start(f32[32,32,1]{2,1,0:T(8,128)} %copy.5002) | copy-start | bytes 12292
  442.1 18.2 %copy-start.39 = (f32[32,32,1]{2,1,0:T(8,128)S(1)}, f32[32,32,1]{2,1,0:T(8,128)}, u32[]{:S(2)}) copy-start(f32[32,32,1]{2,1,0:T(8,128)} %copy.5000) | copy-start | bytes 12292
  442.2 5.9 %collective-permute-start.25 = (f32[2,32,1,128]{3,1,2,0:T(8,128)S(1)}, f32[2,32,1,128]{3,1,2,0:T(8,128)S(1)}, u32[]{:S(2)}, u32[]{:S(2)}) collective-permute-start(f32[2,32,1,128]{3,1,2,0:T(8,128)S(1)} %pad_maximum_fusion.84), channel_id=1, source_target_pairs={{1,0},{2,1},{3,2},{4,3},{5,4},{6,5},{7,6},{8,7},{9,8},{10,9},{11,1... | collective-permute-start | bytes 98312 | tf_op jit(solution)/shard_map/ppermute | solution.py:22
  444.3 4.7 collective-permute-start.24
  449.6 9.7 %collective-permute-start.27 = (f32[2,1,32,128]{3,2,1,0:T(8,128)S(1)}, f32[2,1,32,128]{3,2,1,0:T(8,128)S(1)}, u32[]{:S(2)}, u32[]{:S(2)}) collective-permute-start(f32[2,1,32,128]{3,2,1,0:T(8,128)S(1)} %pad_maximum_fusion.86), channel_id=1, source_target_pairs={{0,16},{16,32},{32,48},{48,64},{64,80},{80,96},{96,112},{1,17},{17... | collective-permute-start | bytes 98312 | tf_op jit(solution)/shard_map/ppermute | solution.py:22
  453.6 6.7 %collective-permute-start.26 = (f32[2,32,1,128]{3,1,2,0:T(8,128)S(1)}, f32[2,32,1,128]{3,1,2,0:T(8,128)S(1)}, u32[]{:S(2)}, u32[]{:S(2)}) collective-permute-start(f32[2,32,1,128]{3,1,2,0:T(8,128)S(1)} %pad_maximum_fusion.85), channel_id=1, source_target_pairs={{0,1},{1,2},{2,3},{3,4},{4,5},{5,6},{6,7},{7,8},{8,9},{9,10},{10,1... | collective-permute-start | bytes 98312 | tf_op jit(solution)/shard_map/ppermute | solution.py:22
  461.2 5.8 %collective-permute-start.29 = (f32[2,32,1,128]{3,1,2,0:T(8,128)S(1)}, f32[2,32,1,128]{3,1,2,0:T(8,128)S(1)}, u32[]{:S(2)}, u32[]{:S(2)}) collective-permute-start(f32[2,32,1,128]{3,1,2,0:T(8,128)S(1)} %pad_maximum_fusion.88), channel_id=1, source_target_pairs={{1,0},{2,1},{3,2},{4,3},{5,4},{6,5},{7,6},{8,7},{9,8},{10,9},{11,1... | collective-permute-start | bytes 98312 | tf_op jit(solution)/shard_map/ppermute | solution.py:22
  463.1 4.7 collective-permute-start.28
  469.0 9.0 %collective-permute-start.31 = (f32[2,1,32,128]{3,2,1,0:T(8,128)S(1)}, f32[2,1,32,128]{3,2,1,0:T(8,128)S(1)}, u32[]{:S(2)}, u32[]{:S(2)}) collective-permute-start(f32[2,1,32,128]{3,2,1,0:T(8,128)S(1)} %pad_maximum_fusion.90), channel_id=1, source_target_pairs={{0,16},{16,32},{32,48},{48,64},{64,80},{80,96},{96,112},{1,17},{17... | collective-permute-start | bytes 98312 | tf_op jit(solution)/shard_map/ppermute | solution.py:22
  472.3 6.7 %collective-permute-start.30 = (f32[2,32,1,128]{3,1,2,0:T(8,128)S(1)}, f32[2,32,1,128]{3,1,2,0:T(8,128)S(1)}, u32[]{:S(2)}, u32[]{:S(2)}) collective-permute-start(f32[2,32,1,128]{3,1,2,0:T(8,128)S(1)} %pad_maximum_fusion.89), channel_id=1, source_target_pairs={{0,1},{1,2},{2,3},{3,4},{4,5},{5,6},{6,7},{7,8},{8,9},{9,10},{10,1... | collective-permute-start | bytes 98312 | tf_op jit(solution)/shard_map/ppermute | solution.py:22
  484.6 50.8 %copy-start.3 = (f32[32,32,128]{2,1,0:T(8,128)S(1)}, f32[32,32,128]{2,1,0:T(8,128)}, u32[]{:S(2)}) copy-start(f32[32,32,128]{2,1,0:T(8,128)} %copy-done.2) | copy-start | bytes 1572868
  484.6 61.7 %copy-start.46 = (f32[128,16]{1,0:T(8,128)S(1)}, f32[128,16]{1,0:T(8,128)}, u32[]{:S(2)}) copy-start(f32[128,16]{1,0:T(8,128)} %copy.5016) | copy-start | bytes 24580
  513.0 32.4 %all-to-all-start.2 = ((f32[128,2,16]{2,1,0:T(2,128)}), f32[128,2,16]{2,1,0:T(2,128)S(1)}, u32[]{:S(2)}, u32[]{:S(2)}) async-start(f32[128,2,16]{2,1,0:T(2,128)} %reshape.462), calls=%async_computation.2 | async-start | bytes 262144 | tf_op jit(solution)/shard_map/all_to_all | solution.py:194
  (43 other events, 381.5 us)
Sparse Core Ops, SparseCore 0:
  170.2 86.0 all-reduce.45
  258.8 143.6 all-reduce.47
